TPU v7x, 256 devices: a whole 4x4x8 slice. The times are simulated.
256 devices in a mesh: term: 8 (over y, core), pass: 32 (over x, z).
Axes of the slice: x: 4, y: 4, z: 8, core: 2. Of those that a mesh axis runs over, the one named last changes fastest.
Arguments:
- hidden: bfloat16 [16384, 4096], P('pass', 'term'), may hold values from -16 to 16
- head_weight: bfloat16 [4096, 16384], P('pass', 'term'), may hold values from -0.09375 to 0.09375
- lengths: int32 [256], P('pass'), may hold values from 1 to 64, as said below
Outputs:
- postings: bfloat16 [16384, 256], P(('term', 'pass'))
Inputs may be any that keep to these rules, and one draw needn't show every extreme that they name: Passage p's valid tokens are its first lengths[p] slots; some passage has exactly 64.
All inputs are finite; a program needn't handle non-finite values.
Results may differ from a plain program's by a relative error of at most 0.013.
Values may be sent and summed in bfloat16 or wider, within the bound.
No kernel may reach another device: no remote copies, remote signals or barrier semaphores. Data moves between devices by JAX's collectives and lax.ppermute only.
A program may use at most 64 MiB of HBM per device.

v0:
```python
import jax
import jax.numpy as jnp
from jax import lax
from jax.sharding import PartitionSpec as P


def body(hidden, head_weight, lengths):
    gathered = lax.all_gather(hidden, "term", axis=1, tiled=True)
    passages = lengths.shape[0]
    tokens_per = gathered.shape[0] // passages
    slab_cols = head_weight.shape[1]
    allowed = jnp.arange(tokens_per, dtype=jnp.int32)[None, :] < lengths[:, None]
    logits = jnp.dot(
        gathered,
        lax.all_gather(head_weight, "pass", axis=0, tiled=True),
        preferred_element_type=jnp.float32,
    )
    impacts = jnp.log1p(jnp.maximum(logits, jnp.float32(0.0)))
    impacts = impacts.reshape(passages, tokens_per, slab_cols)
    impacts = jnp.where(allowed[:, :, None], impacts, jnp.float32(0.0))
    pooled = jnp.max(impacts, axis=1).astype(jnp.bfloat16)
    owners = lax.axis_size("pass")
    range_cols = slab_cols // owners
    local_max = jnp.max(pooled.astype(jnp.float32), axis=0)
    column_max = lax.pmax(local_max, "pass")
    payload = (pooled.astype(jnp.float32) / (1.0 + column_max)[None, :]).astype(jnp.bfloat16)
    shaped = payload.reshape(passages, owners, range_cols)
    return jnp.transpose(
        lax.all_to_all(shaped, "pass", split_axis=1, concat_axis=0, tiled=True)[:, 0, :]
    )


def solution(mesh):
    return jax.shard_map(
        body,
        mesh=mesh,
        in_specs=(P("pass", "term"), P("pass", "term"), P("pass")),
        out_specs=P(("term", "pass"), None),
        check_vma=False,
    )
```

profile of v0, /device:TPU:8, one launch (start us, length us, event | category | flops | bytes accessed | tf_op | source)
XLA Modules:
  0.0 297.9 jit_solution(6542916140701454250)
XLA Ops:
  6.5 0.0 all-gather.3.cloned.1.call-start
  6.5 0.7 all-gather.3.cloned.1.call-update
  7.3 0.0 all-gather.5.cloned.1.call-start
  7.3 0.7 all-gather.5.cloned.1.call-update
  8.0 0.7 iota_compare_fusion
  8.7 37.0 %all-gather.3.cloned.1.call-done = bf16[512,4096]{1,0:T(8,128)(2,1)} async-done(((bf16[512,512]{1,0:T(8,128)(2,1)}), bf16[512,4096]{1,0:T(8,128)(2,1)}) %all-gather.3.cloned.1.call-update) | async-done | bytes 4194320 | tf_op jit(solution)/shard_map/all_gather | solution.py:8
  45.8 144.1 %all-gather.5.cloned.1.call-done = bf16[4096,2048]{1,0:T(8,128)(2,1)} async-done(((bf16[128,2048]{1,0:T(8,128)(2,1)}), bf16[4096,2048]{1,0:T(8,128)(2,1)}) %all-gather.5.cloned.1.call-update) | async-done | bytes 16777232 | tf_op jit(solution)/shard_map/all_gather | solution.py:15
  189.9 14.8 %select_reduce_fusion = bf16[8,2048]{1,0:T(8,128)(2,1)S(1)} fusion(pred[8,64]{1,0:T(8,128)(4,1)S(1)} %iota_compare_fusion, bf16[512,4096]{1,0:T(8,128)(2,1)} %all-gather.3.cloned.1.call-done, bf16[4096,2048]{1,0:T(8,128)(2,1)} %all-gather.5.cloned.1.call-done), kind=kOutput, calls=%fused_computation | convolution fusion | flops 8594112512 | bytes 21004800 | tf_op jit(solution)/shard_map/dot_general | solution.py:13
  204.8 0.1 reshape.37
  204.9 72.3 %pmax.7 = f32[2048]{0:T(1024)S(1)} all-reduce(bf16[2048]{0:T(1024)(128)(2,1)S(1)} %convert_reduce_fusion), channel_id=1, replica_groups=mesh['term'=8,'pass'=32] {'pass'}, use_global_device_ids=true, to_apply=%region_2.3 | all-reduce | flops 2048 | bytes 12288 | tf_op jit(solution)/shard_map/pmax | solution.py:25
  277.2 0.1 div.11
  277.3 0.1 reshape.38
  277.4 12.8 %all_to_all.15 = bf16[32,2,256]{2,1,0:T(2,128)(2,1)S(1)} all-to-all(bf16[32,2,256]{2,1,0:T(2,128)(2,1)S(1)} %reshape.38), channel_id=1, replica_groups=mesh['term'=8,'pass'=32] {'pass'}, dimensions={0} | all-to-all | bytes 65536 | tf_op jit(solution)/shard_map/all_to_all | solution.py:29
  290.2 0.1 reshape.39
  290.4 0.7 copy.7
  (5 shorter events, 0.1 us)
Async XLA Ops:
  6.5 39.2 %all-gather.3.cloned.1.call-start = ((), (), s32[]{:S(2)}) async-start(), calls=%async_computation.1 | async-start | bytes 4718592 | tf_op jit(solution)/shard_map/all_gather | solution.py:8
  7.3 182.6 %all-gather.5.cloned.1.call-start = ((), (), s32[]{:S(2)}) async-start(), calls=%async_computation.2 | async-start | bytes 17301504 | tf_op jit(solution)/shard_map/all_gather | solution.py:15
Sparse Core Ops, SparseCore 0:
  9.2 36.5 all-gather.2
  48.4 141.4 all-gather.4
where the time goes:
time: 298 us
  waiting for transfers between devices  183 us (61%)
  blocking collectives  85.1 us (29%)
  matrix products  14.8 us (5%)
  between operations  13.5 us (5%)
    all_gather x1, waiting for transfers between devices, body(): lax.all_gather(head_weight, 'pass', axis=0, tiled=True)  144 us
    pmax x1, blocking collectives, body(): column_max = lax.pmax(local_max, 'pass')  72.3 us
    all_gather x1, waiting for transfers between devices, body(): gathered = lax.all_gather(hidden, 'term', axis=1, tiled=True)  37 us
    dot_general x1, matrix products, body(): jnp.dot(gathered, lax.all_gather(head_weight, 'pass', axis=0, tiled=True)...  14.8 us
    all_to_all x1, blocking collectives, body(): lax.all_to_all(shaped, 'pass', split_axis=1, concat_axis=0, tiled=True)  12.8 us
  transfers between devices with their start and end apart: 2, of which 2 were waited for; matrix products, arithmetic and copies ran while one was open for 0% of the time, Pallas kernels for 0%

commit v1 on v0

--- a/solution.py
+++ b/solution.py
@@ -4,8 +4,29 @@
 from jax.sharding import PartitionSpec as P
 
 
+def collect(value, axis, dim):
+    length, position, rows = (lax.axis_size(axis), lax.axis_index(axis), value.shape[dim])
+    forward = [(i, (i + 1) % length) for i in range(length)]
+    downward = [(i, (i - 1) % length) for i in range(length)]
+    out = jnp.zeros((*value.shape[:dim], length * rows, *value.shape[dim + 1 :]), value.dtype)
+    out = lax.dynamic_update_slice_in_dim(out, value, position * rows, axis=dim)
+    from_left = from_right = value
+    half = length // 2
+    for step in range(1, half + 1):
+        from_left = lax.ppermute(from_left, axis, forward)
+        out = lax.dynamic_update_slice_in_dim(
+            out, from_left, (position - step) % length * rows, axis=dim
+        )
+        if step < length - half:
+            from_right = lax.ppermute(from_right, axis, downward)
+            out = lax.dynamic_update_slice_in_dim(
+                out, from_right, (position + step) % length * rows, axis=dim
+            )
+    return out
+
+
 def body(hidden, head_weight, lengths):
-    gathered = lax.all_gather(hidden, "term", axis=1, tiled=True)
+    gathered = collect(hidden, "term", 1)
     passages = lengths.shape[0]
     tokens_per = gathered.shape[0] // passages
     slab_cols = head_weight.shape[1]

time: 298 us -> 262 us (0.88)
  waiting for transfers between devices: 183 us -> 132 us
  local copies, waits for them, and re-layouts: 1.16 us -> 10.7 us
  starting transfers between devices: 0.04 us -> 5.48 us
    all_gather x1 -> x0, waiting for transfers between devices: 37 us -> none  [body(): gathered = lax.all_gather(hidden, 'term', axis=1, tiled=True)]
    all_gather x1, waiting for transfers between devices: 144 us -> 111 us  [body(): lax.all_gather(head_weight, 'pass', axis=0, tiled=True)]
    ppermute x0 -> x7, waiting for transfers between devices: none -> 20.4 us  [the longest x4 20.4 us: collect(): from_left = lax.ppermute(from_left, axis, forward)]
    dynamic_update_slice x0 -> x8, local copies, waits for them, and re-layouts: none -> 7.12 us  [the longest x4 3.51 us: collect(): lax.dynamic_update_slice_in_dim(out, from_left, (position - step) % lengt...]
    ppermute x0 -> x7, starting transfers between devices: none -> 5.48 us  [the longest x3 5.46 us: collect(): from_right = lax.ppermute(from_right, axis, downward)]
  transfers between devices with their start and end apart: 2 -> 8, of which waited for: 2 -> 5; matrix products, arithmetic and copies ran while one was open for 0% -> 4% of each run, Pallas kernels for 0% -> 0%
where the time goes in v1:
time: 262 us; the launch traced here: 261 us
  waiting for transfers between devices  132 us (50%)
  blocking collectives  85.1 us (32%)
  matrix products  14.8 us (6%)
  between operations  13.5 us (5%)
  local copies, waits for them, and re-layouts  10.7 us (4%)
  starting transfers between devices  5.48 us (2%)
    all_gather x1, waiting for transfers between devices, body(): lax.all_gather(head_weight, 'pass', axis=0, tiled=True)  111 us
    pmax x1, blocking collectives, body(): column_max = lax.pmax(local_max, 'pass')  72.3 us
    ppermute x4, waiting for transfers between devices, collect(): from_left = lax.ppermute(from_left, axis, forward)  20.4 us
    dot_general x1, matrix products, body(): jnp.dot(gathered, lax.all_gather(head_weight, 'pass', axis=0, tiled=True)...  14.8 us
    all_to_all x1, blocking collectives, body(): lax.all_to_all(shaped, 'pass', split_axis=1, concat_axis=0, tiled=True)  12.8 us
    ppermute x3, starting transfers between devices, collect(): from_right = lax.ppermute(from_right, axis, downward)  5.46 us
  transfers between devices with their start and end apart: 8, of which 5 were waited for; matrix products, arithmetic and copies ran while one was open for 4% of the time, Pallas kernels for 0%

profile of v1, /device:TPU:8, one launch (start us, length us, event | category | flops | bytes accessed | tf_op | source)
XLA Modules:
  0.0 261.4 jit_solution(2563005967418677957)
XLA Ops:
  6.5 0.0 copy-start
  6.5 0.0 copy-start.1
  6.5 0.0 all-gather.2.cloned.1.call-start
  6.5 0.7 all-gather.2.cloned.1.call-update
  7.3 0.0 collective-permute-start
  7.3 1.7 collective-permute-start.1
  9.0 7.1 %collective-permute-done = bf16[512,512]{1,0:T(8,128)(2,1)S(1)} collective-permute-done((bf16[512,512]{1,0:T(8,128)(2,1)}, bf16[512,512]{1,0:T(8,128)(2,1)S(1)}, u32[]{:S(2)}, u32[]{:S(2)}) %collective-permute-start) | collective-permute-done | bytes 524320 | tf_op jit(solution)/shard_map/ppermute | solution.py:16
  16.1 0.0 collective-permute-start.2
  16.1 0.0 collective-permute-done.1
  16.1 2.0 collective-permute-start.3
  18.1 6.6 %collective-permute-done.2 = bf16[512,512]{1,0:T(8,128)(2,1)S(1)} collective-permute-done((bf16[512,512]{1,0:T(8,128)(2,1)S(1)}, bf16[512,512]{1,0:T(8,128)(2,1)S(1)}, u32[]{:S(2)}, u32[]{:S(2)}) %collective-permute-start.2) | collective-permute-done | bytes 524320 | tf_op jit(solution)/shard_map/ppermute | solution.py:16
  24.7 0.0 collective-permute-start.4
  24.7 2.4 broadcast_in_dim.20
  27.1 0.0 copy-done
  27.2 0.9 constant_dynamic-update-slice_fusion.7
  28.1 0.0 copy-done.1
  28.1 0.1 iota_compare_fusion
  28.1 0.0 collective-permute-done.3
  28.1 1.7 collective-permute-start.5
  29.8 0.9 constant_dynamic-update-slice_fusion.6
  30.7 2.6 collective-permute-done.4
  33.3 0.0 collective-permute-start.6
  33.3 0.9 constant_dynamic-update-slice_fusion.5
  34.2 0.9 constant_dynamic-update-slice_fusion.4
  35.1 0.9 constant_dynamic-update-slice_fusion.3
  35.9 0.9 constant_dynamic-update-slice_fusion.2
  36.8 0.0 collective-permute-done.5
  36.8 0.9 constant_dynamic-update-slice_fusion.1
  37.7 4.2 %collective-permute-done.6 = bf16[512,512]{1,0:T(8,128)(2,1)S(1)} collective-permute-done((bf16[512,512]{1,0:T(8,128)(2,1)S(1)}, bf16[512,512]{1,0:T(8,128)(2,1)S(1)}, u32[]{:S(2)}, u32[]{:S(2)}) %collective-permute-start.6) | collective-permute-done | bytes 524320 | tf_op jit(solution)/shard_map/ppermute | solution.py:16
  41.9 0.9 constant_dynamic-update-slice_fusion
  42.8 110.6 %all-gather.2.cloned.1.call-done = bf16[4096,2048]{1,0:T(8,128)(2,1)} async-done(((bf16[128,2048]{1,0:T(8,128)(2,1)}), bf16[4096,2048]{1,0:T(8,128)(2,1)}) %all-gather.2.cloned.1.call-update) | async-done | bytes 16777232 | tf_op jit(solution)/shard_map/all_gather | solution.py:36
  153.4 14.8 %select_reduce_fusion = bf16[8,2048]{1,0:T(8,128)(2,1)S(1)} fusion(pred[8,64]{1,0:T(8,128)(4,1)S(1)} %iota_compare_fusion, bf16[512,4096]{1,0:T(8,128)(2,1)} %constant_dynamic-update-slice_fusion, bf16[4096,2048]{1,0:T(8,128)(2,1)} %all-gather.2.cloned.1.call-done), kind=kOutput, calls=%fused_computation | convolution fusion | flops 8594112512 | bytes 21004800 | tf_op jit(solution)/shard_map/dot_general | solution.py:34
  168.2 0.1 reshape.37
  168.3 72.3 %pmax.7 = f32[2048]{0:T(1024)S(1)} all-reduce(bf16[2048]{0:T(1024)(128)(2,1)S(1)} %convert_reduce_fusion), channel_id=1, replica_groups=mesh['term'=8,'pass'=32] {'pass'}, use_global_device_ids=true, to_apply=%region_2.3 | all-reduce | flops 2048 | bytes 12288 | tf_op jit(solution)/shard_map/pmax | solution.py:46
  240.7 0.1 div.11
  240.8 0.1 reshape.38
  240.9 12.8 %all_to_all.15 = bf16[32,2,256]{2,1,0:T(2,128)(2,1)S(1)} all-to-all(bf16[32,2,256]{2,1,0:T(2,128)(2,1)S(1)} %reshape.38), channel_id=1, replica_groups=mesh['term'=8,'pass'=32] {'pass'}, dimensions={0} | all-to-all | bytes 65536 | tf_op jit(solution)/shard_map/all_to_all | solution.py:50
  253.7 0.1 reshape.39
  253.8 0.7 copy.7
  (5 shorter events, 0.1 us)
Async XLA Ops:
  6.5 20.6 %copy-start = (bf16[512,512]{1,0:T(8,128)(2,1)S(1)}, bf16[512,512]{1,0:T(8,128)(2,1)}, u32[]{:S(2)}) copy-start(bf16[512,512]{1,0:T(8,128)(2,1)} %param.3) | copy-start | bytes 1572868
  6.5 21.5 %copy-start.1 = (s32[8]{0:T(128)S(1)}, s32[8]{0:T(128)}, u32[]{:S(2)}) copy-start(s32[8]{0:T(128)} %param.5) | copy-start | bytes 100
  6.5 146.8 %all-gather.2.cloned.1.call-start = ((), (), s32[]{:S(2)}) async-start(), calls=%async_computation.1 | async-start | bytes 17301504 | tf_op jit(solution)/shard_map/all_gather | solution.py:36
  7.3 8.8 %collective-permute-start = (bf16[512,512]{1,0:T(8,128)(2,1)}, bf16[512,512]{1,0:T(8,128)(2,1)S(1)}, u32[]{:S(2)}, u32[]{:S(2)}) collective-permute-start(bf16[512,512]{1,0:T(8,128)(2,1)} %param.3), channel_id=1, source_target_pairs={{0,32},{32,64},{64,96},{96,128},{128,160},{160,192},{192,224},{224... | collective-permute-start | bytes 1572872 | tf_op jit(solution)/shard_map/ppermute | solution.py:16
  7.3 8.8 %collective-permute-start.1 = (bf16[512,512]{1,0:T(8,128)(2,1)}, bf16[512,512]{1,0:T(8,128)(2,1)S(1)}, u32[]{:S(2)}, u32[]{:S(2)}) collective-permute-start(bf16[512,512]{1,0:T(8,128)(2,1)} %param.3), channel_id=1, source_target_pairs={{0,224},{32,0},{64,32},{96,64},{128,96},{160,128},{192,160},{224,1... | collective-permute-start | bytes 1572872 | tf_op jit(solution)/shard_map/ppermute | solution.py:21
  16.1 8.6 %collective-permute-start.2 = (bf16[512,512]{1,0:T(8,128)(2,1)S(1)}, bf16[512,512]{1,0:T(8,128)(2,1)S(1)}, u32[]{:S(2)}, u32[]{:S(2)}) collective-permute-start(bf16[512,512]{1,0:T(8,128)(2,1)S(1)} %collective-permute-done), channel_id=1, source_target_pairs={{0,32},{32,64},{64,96},{96,128},{128,160},{160,192},{192,224},{224... | collective-permute-start | bytes 1572872 | tf_op jit(solution)/shard_map/ppermute | solution.py:16
  16.1 12.1 %collective-permute-start.3 = (bf16[512,512]{1,0:T(8,128)(2,1)S(1)}, bf16[512,512]{1,0:T(8,128)(2,1)S(1)}, u32[]{:S(2)}, u32[]{:S(2)}) collective-permute-start(bf16[512,512]{1,0:T(8,128)(2,1)S(1)} %collective-permute-done.1), channel_id=1, source_target_pairs={{0,224},{32,0},{64,32},{96,64},{128,96},{160,128},{192,160},{224,1... | collective-permute-start | bytes 1572872 | tf_op jit(solution)/shard_map/ppermute | solution.py:21
  24.7 8.6 %collective-permute-start.4 = (bf16[512,512]{1,0:T(8,128)(2,1)S(1)}, bf16[512,512]{1,0:T(8,128)(2,1)S(1)}, u32[]{:S(2)}, u32[]{:S(2)}) collective-permute-start(bf16[512,512]{1,0:T(8,128)(2,1)S(1)} %collective-permute-done.2), channel_id=1, source_target_pairs={{0,32},{32,64},{64,96},{96,128},{128,160},{160,192},{192,224},{224... | collective-permute-start | bytes 1572872 | tf_op jit(solution)/shard_map/ppermute | solution.py:16
  28.1 8.7 %collective-permute-start.5 = (bf16[512,512]{1,0:T(8,128)(2,1)S(1)}, bf16[512,512]{1,0:T(8,128)(2,1)S(1)}, u32[]{:S(2)}, u32[]{:S(2)}) collective-permute-start(bf16[512,512]{1,0:T(8,128)(2,1)S(1)} %collective-permute-done.3), channel_id=1, source_target_pairs={{0,224},{32,0},{64,32},{96,64},{128,96},{160,128},{192,160},{224,1... | collective-permute-start | bytes 1572872 | tf_op jit(solution)/shard_map/ppermute | solution.py:21
  33.3 8.6 %collective-permute-start.6 = (bf16[512,512]{1,0:T(8,128)(2,1)S(1)}, bf16[512,512]{1,0:T(8,128)(2,1)S(1)}, u32[]{:S(2)}, u32[]{:S(2)}) collective-permute-start(bf16[512,512]{1,0:T(8,128)(2,1)S(1)} %collective-permute-done.4), channel_id=1, source_target_pairs={{0,32},{32,64},{64,96},{96,128},{128,160},{160,192},{192,224},{224... | collective-permute-start | bytes 1572872 | tf_op jit(solution)/shard_map/ppermute | solution.py:16
Sparse Core Ops, SparseCore 0:
  10.0 143.3 all-gather.1
